TPU v7x, 256 devices: a whole 4x4x8 slice. The times are simulated.
256 devices in a mesh: seq: 32 (over x, y, core), head: 8 (over z).
Axes of the slice: x: 4, y: 4, z: 8, core: 2. Of those that a mesh axis runs over, the one named last changes fastest.
Arguments:
- tokens: bfloat16 [32768, 2048], P('seq', 'head'), may hold values from -6 to 6
- seg_ids: int32 [32768], replicated, may hold values from 0 to 31, never falling along the last dimension, each value on 1 to 16384 neighbouring positions
- w_gate: bfloat16 [2048, 4096], P(None, 'head'), may hold values from -0.125 to 0.125
- w_x: bfloat16 [2048, 4096], P(None, 'head'), may hold values from -0.125 to 0.125
- w_bc: bfloat16 [2048, 256], replicated, may hold values from -0.125 to 0.125
- w_dt: bfloat16 [2048, 64], P(None, 'head'), may hold values from -0.125 to 0.125
- conv_x: float32 [4, 4096], P(None, 'head'), may hold values from -3 to 3
- conv_bc: float32 [4, 256], replicated, may hold values from -3 to 3
- conv_x_bias: float32 [4096], P('head'), may hold values from -3 to 3
- conv_bc_bias: float32 [256], replicated, may hold values from -3 to 3
- dt_bias: float32 [64], P('head'), may hold values from -4 to -1
- decay_rate: float32 [64], P('head'), may hold values from 0.0002 to 4
- skip_gain: float32 [64], P('head'), may hold values from 0.5 to 1.5
- norm_gain: float32 [4096], P('head'), may hold values from 0.5 to 1.5
- w_out: bfloat16 [4096, 2048], P('head'), may hold values from -0.125 to 0.125
Outputs:
- mixed: bfloat16 [32768, 2048], P('seq', 'head')
- end_state: float32 [32, 64, 64, 128], P('seq', 'head')
Inputs may be any that keep to these rules, and one draw needn't show every extreme that they name: `seg_ids`: prompt numbers never fall along the tokens; each prompt holds 1 to 16384 tokens, one of them exactly 16384.
All inputs are finite; a program needn't handle non-finite values.
Results may differ from a plain program's by a relative error of at most 0.0075.
Values may be sent and summed in bfloat16 or wider, within the bound.
A program may use at most 128 MiB of HBM per device.

v0:
```python
import jax
import jax.numpy as jnp
from jax import lax
from jax.sharding import PartitionSpec as P

GROUP = 256
INNER = 4096
EPSILON = 1e-05
HIGH = lax.Precision.HIGHEST


def shifted(x, axis, by):
    devices = lax.axis_size(axis)
    pairs = [(i, i + by) for i in range(devices) if 0 <= i + by < devices]
    return lax.ppermute(x, axis, pairs)


def carried_in(part, axis, combine, identity):
    place = lax.axis_index(axis)
    gathered = jax.tree.map(lambda a: lax.all_gather(a, axis), part)
    state = jax.tree.map(lambda a, e: jnp.zeros_like(a) + jnp.asarray(e, a.dtype), part, identity)

    def one(hop, state):
        return combine(
            state, jax.tree.map(lambda a: lax.dynamic_index_in_dim(a, hop, 0, False), gathered)
        )

    return lax.fori_loop(0, place, one, state)


def conv_block(projected, edge_rows, weights, offsets, idents, earlier):
    rows_here = projected.shape[0]
    lag_count = edge_rows.shape[0]
    joined = jnp.concatenate([edge_rows, projected], 0).astype(jnp.float32)
    joined_ids = jnp.concatenate([earlier, idents], 0)
    result = joined[lag_count:] * weights[0]
    for shift_by in range(1, lag_count + 1):
        window = joined[lag_count - shift_by : lag_count - shift_by + rows_here]
        matches = joined_ids[lag_count - shift_by : lag_count - shift_by + rows_here] == idents
        result = result + jnp.where(matches[:, None], window, 0.0) * weights[shift_by]
    return result + offsets


def combine(earlier, later):
    return (earlier[0] * later[0], later[0][:, None, None] * earlier[1] + later[1])


def shards(
    tokens,
    seg_ids,
    w_gate,
    w_x,
    w_bc,
    w_dt,
    conv_x,
    conv_bc,
    conv_x_bias,
    conv_bc_bias,
    dt_bias,
    decay_rate,
    skip_gain,
    norm_gain,
    w_out,
):
    rows_here = tokens.shape[0]
    heads_here = w_dt.shape[1]
    inner_here = w_x.shape[1]
    head_width = inner_here // heads_here
    state_width = w_bc.shape[1] // 2
    lag_count = conv_x.shape[0] - 1
    device = lax.axis_index("seq")
    first_row = device * rows_here
    piece = lax.all_gather(tokens, "head", axis=1, tiled=True)

    def partial_product(matrix):
        return jnp.dot(piece, matrix, preferred_element_type=jnp.float32)

    gate_full = partial_product(w_gate)
    x_sum = partial_product(w_x)
    bc_sum = partial_product(w_bc)
    dt_raw = partial_product(w_dt)
    x_pre = x_sum.astype(jnp.bfloat16)
    bc_pre = bc_sum.astype(jnp.bfloat16)
    idents = lax.dynamic_slice_in_dim(seg_ids, first_row, rows_here)
    earlier = lax.dynamic_slice_in_dim(seg_ids, jnp.maximum(first_row - lag_count, 0), lag_count)
    earlier = jnp.where(device > 0, earlier, -1)
    edge_x, edge_bc = shifted(
        (x_pre[rows_here - lag_count :], bc_pre[rows_here - lag_count :]), "seq", 1
    )
    x_conv = jax.nn.silu(conv_block(x_pre, edge_x, conv_x, conv_x_bias, idents, earlier)).astype(
        jnp.bfloat16
    )
    bc_conv = jax.nn.silu(
        conv_block(bc_pre, edge_bc, conv_bc, conv_bc_bias, idents, earlier)
    ).astype(jnp.bfloat16)
    steps_dt = jax.nn.softplus(dt_raw + dt_bias)
    log_decay = -steps_dt * decay_rate
    x_float = x_conv.astype(jnp.float32).reshape(rows_here, heads_here, head_width)
    x_scaled = x_float * steps_dt[:, :, None]
    count = rows_here // GROUP
    group_x = x_scaled.reshape(count, GROUP, heads_here, head_width)
    group_b = bc_conv[:, :state_width].astype(jnp.float32).reshape(count, GROUP, state_width)
    group_c = bc_conv[:, state_width:].astype(jnp.float32).reshape(count, GROUP, state_width)
    group_ids = idents.reshape(count, GROUP)
    cumul = jnp.cumsum(log_decay.reshape(count, GROUP, heads_here), axis=1)
    cumul_heads = jnp.transpose(cumul, (0, 2, 1))
    places = jnp.arange(GROUP)
    causal = places[None, :] <= places[:, None]
    linked = causal[None] & (group_ids[:, :, None] == group_ids[:, None, :])
    gaps = cumul_heads[:, :, :, None] - cumul_heads[:, :, None, :]
    link_heads = linked[:, None, :, :]
    decays = jnp.where(link_heads, jnp.exp(jnp.where(link_heads, gaps, 0.0)), 0.0)
    scores = jnp.einsum("ctn,csn->cts", group_c, group_b, precision=HIGH)
    within = jnp.einsum("chts,cshp->cthp", decays * scores[:, None, :, :], group_x, precision=HIGH)
    last_ids = group_ids[:, -1]
    tails = jnp.where(
        (group_ids == last_ids[:, None])[:, :, None], jnp.exp(cumul[:, -1:, :] - cumul), 0.0
    )
    group_states = jnp.einsum(
        "cshp,csn->chpn", group_x * tails[:, :, :, None], group_b, precision=HIGH
    )
    prior_ids = jnp.concatenate([earlier[-1:], last_ids[:-1]], 0)
    passing = jnp.where((last_ids == prior_ids)[:, None], jnp.exp(cumul[:, -1, :]), 0.0)
    local_list = []
    gain_list = []
    running_state = jnp.zeros((heads_here, head_width, state_width), jnp.float32)
    running_gain = jnp.ones((heads_here,), jnp.float32)
    for group_no in range(count):
        local_list.append(running_state)
        gain_list.append(running_gain)
        running_state = passing[group_no][:, None, None] * running_state + group_states[group_no]
        running_gain = passing[group_no] * running_gain
    identity = (jnp.ones_like(running_gain), jnp.zeros_like(running_state))
    prefix_gain, incoming = carried_in((running_gain, running_state), "seq", combine, identity)
    entering = jnp.stack(gain_list, 0)[:, :, None, None] * incoming[None] + jnp.stack(local_list, 0)
    enter_weight = jnp.where((group_ids == prior_ids[:, None])[:, :, None], jnp.exp(cumul), 0.0)
    carried = (
        jnp.einsum("ctn,chpn->cthp", group_c, entering, precision=HIGH)
        * enter_weight[:, :, :, None]
    )
    end_state = (running_gain[:, None, None] * incoming + running_state)[None]
    ssd_out = (within + carried).reshape(rows_here, heads_here, head_width) + skip_gain[
        None, :, None
    ] * x_float
    gated = ssd_out.reshape(rows_here, inner_here) * jax.nn.silu(gate_full)
    square_total = lax.psum(jnp.sum(gated * gated, axis=1), "head")
    mean_square = (square_total / INNER)[:, None]
    hidden = (gated * lax.rsqrt(mean_square + EPSILON) * norm_gain).astype(jnp.bfloat16)
    partial_out = jnp.dot(hidden, w_out, preferred_element_type=jnp.float32)
    mixed = lax.psum_scatter(partial_out, "head", scatter_dimension=1, tiled=True).astype(
        jnp.bfloat16
    )
    return (mixed, end_state)


def solution(mesh):
    return jax.shard_map(
        shards,
        mesh=mesh,
        in_specs=(
            P("seq", "head"),
            P(),
            P(None, "head"),
            P(None, "head"),
            P(),
            P(None, "head"),
            P(None, "head"),
            P(),
            P("head"),
            P(),
            P("head"),
            P("head"),
            P("head"),
            P("head"),
            P("head", None),
        ),
        out_specs=(P("seq", "head"), P("seq", "head", None, None)),
        check_vma=False,
    )
```

profile of v0, /device:TPU:1, one launch (start us, length us, event | category | flops | bytes accessed | tf_op | source)
XLA Modules:
  0.0 347.8 jit_solution(15108138510818791325)
XLA Ops:
  7.2 0.7 all-gather.4.cloned.1.call-update
  8.0 0.7 dynamic_slice.17
  8.7 0.8 broadcast_select_fusion
  9.4 0.6 slice.151
  10.0 0.2 fusion.60
  10.2 0.7 pad_add_fusion.1
  10.9 0.2 slice_reduce_fusion.1
  11.1 0.8 fusion.53
  12.1 0.8 fusion.61
  12.9 0.9 fusion.59
  13.8 58.4 %all-gather.4.cloned.1.call-done = bf16[1024,2048]{1,0:T(8,128)(2,1)} async-done(((bf16[1024,256]{1,0:T(8,128)(2,1)}), bf16[1024,2048]{1,0:T(8,128)(2,1)}) %all-gather.4.cloned.1.call-update) | async-done | bytes 4194320 | tf_op jit(solution)/shard_map/all_gather | solution.py:73
  72.3 3.9 %convolution_convert_fusion.1 = bf16[1024,256]{1,0:T(8,128)(2,1)S(1)} fusion(bf16[1024,2048]{1,0:T(8,128)(2,1)} %all-gather.4.cloned.1.call-done, bf16[2048,256]{1,0:T(8,128)(2,1)} %param.21), kind=kOutput, calls=%fused_computation.33 | convolution fusion | flops 1074003968 | bytes 5767168 | tf_op jit(solution)/shard_map/dot_general | solution.py:76
  76.2 7.4 %collective-permute-start.1 = (bf16[3,256]{1,0:T(4,128)(2,1)S(1)}, bf16[3,256]{1,0:T(4,128)(2,1)S(1)}, u32[]{:S(2)}, u32[]{:S(2)}) collective-permute-start(bf16[3,256]{1,0:T(4,128)(2,1)S(1)} %slice.175), channel_id=1, source_target_pairs={{0,8},{8,16},{16,24},{24,32},{32,40},{40,48},{48,56},{56,64},{64,7... | collective-permute-start | bytes 4616 | tf_op jit(solution)/shard_map/ppermute | solution.py:15
  83.6 1.2 negate_multiply_fusion
  84.8 2.3 reduce-window.6
  87.2 0.1 copy.66
  87.3 0.1 exponential_select_fusion
  87.4 0.2 slice_reduce_fusion
  87.6 0.1 exponential_select_fusion.1
  87.7 5.2 %convolution_convert_fusion = bf16[1024,512]{1,0:T(8,128)(2,1)S(1)} fusion(bf16[1024,2048]{1,0:T(8,128)(2,1)} %all-gather.4.cloned.1.call-done, bf16[2048,512]{1,0:T(8,128)(2,1)} %param.20), kind=kOutput, calls=%fused_computation.32 | convolution fusion | flops 2148007936 | bytes 7340032 | tf_op jit(solution)/shard_map/dot_general | solution.py:76
  93.0 1.9 collective-permute-start
  95.0 0.1 maximum_convert_fusion.1
  95.1 1.3 multiply_convert_fusion.3
  96.4 0.7 fusion.58
  97.2 0.3 maximum_convert_fusion
  97.5 3.1 fusion.37
  100.7 2.9 copy.64
  103.6 3.2 reshape.162
  106.8 3.8 %broadcast_multiply_fusion = (f32[4,256,8,64]{1,0,3,2:T(4,128)S(1)}, f32[4,256,8,64]{1,0,3,2:T(4,128)}) fusion(f32[4,256,8]{1,0,2:T(4,128)S(1)} %copy.69, f32[4,256,8,64]{1,0,3,2:T(4,128)} %reshape.162, f32[4,256,8]{1,0,2:T(4,128)S(1)} %copy.65), kind=kLoop, calls=%fused_computation.57 | loop fusion | flops 1048576 | bytes 6356992 | tf_op jit(solution)/shard_map/mul | solution.py:120
  110.6 1.3 fusion.18
  111.9 1.1 multiply_add_fusion
  113.1 0.1 mul.359
  113.2 0.2 compare_and_fusion
  113.5 22.6 %all-gather = f32[32,1,8]{2,1,0:T(1,128)S(1)} all-gather(f32[1,1,8]{2,1,0:T(1,128)S(1)} %get-tuple-element.93), channel_id=1, replica_groups=mesh['seq'=32,'head'=8] {'seq'}, dimensions={0}, use_global_device_ids=true | all-gather | bytes 1056 | tf_op jit(solution)/shard_map/all_gather | solution.py:20
  136.3 1.2 fusion.63
  137.5 12.0 %fusion = f32[4,8,64,256]{3,2,1,0:T(8,128)} fusion(f32[4,256,256]{2,1,0:T(8,128)S(1)} %fusion.63, f32[4,8,256]{2,1,0:T(8,128)S(1)} %add_bitcast_fusion.1, pred[4,256,256]{2,1,0:T(8,128)(4,1)S(1)} %compare_and_fusion, f32[4,256,8,64]{1,0,3,2:T(4,128)} %get-tuple-element.69), kind=kOutput, calls=%fused_computation.2 | convolution fusion | flops 1619001344 | bytes 5537792 | tf_op jit(solution)/shard_map/chts,cshp->cthp/dot_general | solution.py:114
  149.6 20.0 %all-gather.6.cloned.1.call-done = f32[32,8,64,128]{3,2,1,0:T(8,128)} async-done(((f32[1,8,64,128]{3,2,1,0:T(8,128)}), f32[32,8,64,128]{3,2,1,0:T(8,128)}) %all-gather.6.cloned.1.call-update) | async-done | bytes 8388624 | tf_op jit(solution)/shard_map/all_gather | solution.py:20
  169.6 1.1 while.12
  169.6 1.1 bitcast_add_fusion.7
  170.7 4.3 %bitcast_add_fusion.1 = f32[4,256,8,64]{1,3,2,0:T(8,128)} fusion(f32[4,8,64,256]{3,2,1,0:T(8,128)} %fusion, bf16[4,256,128,1]{2,1,3,0:T(8,128)(2,1)} %bitcast.114, f32[1,8,64,128]{3,2,1,0:T(8,128)} %get-tuple-element.60, f32[1,8,64,128]{3,2,1,0:T(8,128)} %get-tuple-element.61, f32[1,8,64,128]{3,2,1,0:T(8,128)} %get-tuple-element.62, ...), kind=kOutput, calls=%fused_computation.24 | convolution fusion | flops 807665664 | bytes 5537936 | tf_op jit(solution)/shard_map/ctn,chpn->cthp/dot_general | solution.py:138
  175.0 3.8 %copy.78 = f32[4,256,8,64]{3,2,1,0:T(8,128)} copy(f32[4,256,8,64]{1,3,2,0:T(8,128)} %bitcast_add_fusion.1) | data formatting | bytes 4194304 | tf_op jit(solution)/shard_map/reshape | solution.py:142
  178.8 4.8 %reshape.173 = f32[1024,512]{1,0:T(8,128)} reshape(f32[4,256,8,64]{3,2,1,0:T(8,128)} %copy.78) | data formatting | bytes 4194304 | tf_op jit(solution)/shard_map/reshape | solution.py:142
  183.6 8.1 %multiply_reduce_fusion = (f32[1024]{0:T(1024)S(1)}, f32[1024,512]{1,0:T(8,128)}) fusion(f32[1024,512]{1,0:T(8,128)} %reshape.173, f32[1024,512]{1,0:T(8,128)} %fusion.37, f32[512]{0:T(512)S(1)} %mul.359, bf16[1024,2048]{1,0:T(8,128)(2,1)} %all-gather.4.cloned.1.call-done, bf16[2048,512]{1,0:T(8,128)(2,1)} %param.19), kind=kOutput, calls=%fused_computation.29 | convolution fusion | flops 2152201216 | bytes 12589056 | tf_op jit(solution)/shard_map/dot_general | solution.py:76
  191.7 13.7 %psum.7 = f32[1024]{0:T(1024)S(1)} all-reduce(f32[1024]{0:T(1024)S(1)} %get-tuple-element.57), channel_id=1, replica_groups=mesh['seq'=32,'head'=8] {'head'}, use_global_device_ids=true, to_apply=%region_5.6 | all-reduce | flops 1024 | bytes 8192 | tf_op jit(solution)/shard_map/psum | solution.py:146
  205.4 7.2 %fusion.21 = f32[1024,2048]{1,0:T(8,128)} fusion(bf16[512,2048]{1,0:T(8,128)(2,1)S(1)} %copy-done, f32[1024,512]{1,0:T(8,128)} %get-tuple-element.58, f32[512]{0:T(512)S(1)} %copy-done.3, f32[1024]{0:T(1024)S(1)} %add_rsqrt_fusion), kind=kOutput, calls=%fused_computation.36 | convolution fusion | flops 2149056512 | bytes 12589056 | tf_op jit(solution)/shard_map/dot_general | solution.py:149
  212.7 0.9 fusion.42
  213.5 125.7 %reduce-scatter.2.cloned.1.call-done = f32[1024,256]{1,0:T(8,128)} async-done(((f32[1024,2048]{1,0:T(8,128)}), f32[1024,256]{1,0:T(8,128)}) %reduce-scatter.2.cloned.1.call-update) | async-done | bytes 1048592 | tf_op jit(solution)/shard_map/reduce_scatter | solution.py:150
  339.2 2.1 convert_element_type.37
  (48 shorter events, 0.9 us)
Async XLA Ops:
  7.2 198.2 %copy-start = (bf16[512,2048]{1,0:T(8,128)(2,1)S(1)}, bf16[512,2048]{1,0:T(8,128)(2,1)}, u32[]{:S(2)}) copy-start(bf16[512,2048]{1,0:T(8,128)(2,1)} %param.31) | copy-start | bytes 6291460
  7.2 65.1 %all-gather.4.cloned.1.call-start = ((), (), s32[]{:S(2)}) async-start(), calls=%async_computation.1 | async-start | bytes 4718592 | tf_op jit(solution)/shard_map/all_gather | solution.py:73
  7.9 161.6 %all-gather.6.cloned.1.call-start = ((), (), s32[]{:S(2)}) async-start(), calls=%async_computation.2 | async-start | bytes 8650752 | tf_op jit(solution)/shard_map/all_gather | solution.py:20
  13.8 69.8 %copy-start.2 = (bf16[2048,8]{0,1:T(8,128)(2,1)S(1)}, bf16[2048,8]{0,1:T(8,128)(2,1)}, u32[]{:S(2)}) copy-start(bf16[2048,8]{0,1:T(8,128)(2,1)} %param.22) | copy-start | bytes 98308
  13.8 69.8 %copy-start.5 = (f32[8]{0:T(128)S(1)}, f32[8]{0:T(128)}, u32[]{:S(2)}) copy-start(f32[8]{0:T(128)} %param.28) | copy-start | bytes 100
  13.8 69.8 %copy-start.6 = (f32[8]{0:T(128)S(1)}, f32[8]{0:T(128)}, u32[]{:S(2)}) copy-start(f32[8]{0:T(128)} %param.27) | copy-start | bytes 100
  72.3 11.3 %copy-start.1 = (bf16[1024,2048]{1,0:T(8,128)(2,1)S(1)}, bf16[1024,2048]{1,0:T(8,128)(2,1)}, u32[]{:S(2)}) copy-start(bf16[1024,2048]{1,0:T(8,128)(2,1)} %all-gather.4.cloned.1.call-done) | copy-start | bytes 12582916
  76.2 18.8 %collective-permute-start.1 = (bf16[3,256]{1,0:T(4,128)(2,1)S(1)}, bf16[3,256]{1,0:T(4,128)(2,1)S(1)}, u32[]{:S(2)}, u32[]{:S(2)}) collective-permute-start(bf16[3,256]{1,0:T(4,128)(2,1)S(1)} %slice.175), channel_id=1, source_target_pairs={{0,8},{8,16},{16,24},{24,32},{32,40},{40,48},{48,56},{56,64},{64,7... | collective-permute-start | bytes 4616 | tf_op jit(solution)/shard_map/ppermute | solution.py:15
  87.7 7.3 %copy-start.7 = (f32[256]{0:T(256)S(1)}, f32[256]{0:T(256)}, u32[]{:S(2)}) copy-start(f32[256]{0:T(256)} %param.26) | copy-start | bytes 3076
  93.0 4.2 %collective-permute-start = (bf16[3,512]{1,0:T(4,128)(2,1)S(1)}, bf16[3,512]{1,0:T(4,128)(2,1)S(1)}, u32[]{:S(2)}, u32[]{:S(2)}) collective-permute-start(bf16[3,512]{1,0:T(4,128)(2,1)S(1)} %slice.164), channel_id=1, source_target_pairs={{0,8},{8,16},{16,24},{24,32},{32,40},{40,48},{48,56},{56,64},{64,7... | collective-permute-start | bytes 9224 | tf_op jit(solution)/shard_map/ppermute | solution.py:15
  96.4 1.1 copy-start.4
  110.6 2.4 copy-start.8
  112.9 226.3 %reduce-scatter.2.cloned.1.call-start = ((), (), s32[]{:S(2)}) async-start(), calls=%async_computation.3 | async-start | bytes 9437184 | tf_op jit(solution)/shard_map/reduce_scatter | solution.py:150
  183.6 21.8 %copy-start.3 = (f32[512]{0:T(512)S(1)}, f32[512]{0:T(512)}, u32[]{:S(2)}) copy-start(f32[512]{0:T(512)} %param.30) | copy-start | bytes 6148
Sparse Core Ops, SparseCore 0:
  9.7 62.5 all-gather.3
  113.1 56.4 all-gather.5
  212.8 126.4 reduce-scatter.1
where the time goes:
time: 349 us; the launch traced here: 348 us
  waiting for transfers between devices  205 us (59%)
  matrix products  44.5 us (13%)
  blocking collectives  36.3 us (10%)
  local copies, waits for them, and re-layouts  19.5 us (6%)
  other arithmetic  19.2 us (6%)
  between operations  14.1 us (4%)
  starting transfers between devices  9.41 us (3%)
    reduce_scatter x1, waiting for transfers between devices, shards(): lax.psum_scatter(partial_out, 'head', scatter_dimension=1, tiled=True)  126 us
    all_gather x1, waiting for transfers between devices, shards(): piece = lax.all_gather(tokens, 'head', axis=1, tiled=True)  58.4 us
    all_gather x1, blocking collectives, carried_in(): gathered = jax.tree.map(lambda a: lax.all_gather(a, axis), part)  22.6 us
    all_gather x1, waiting for transfers between devices, carried_in(): gathered = jax.tree.map(lambda a: lax.all_gather(a, axis), part)  20 us
    dot_general x4, matrix products, partial_product(): return jnp.dot(piece, matrix, preferred_element_type=jnp.float32)  18.4 us
    psum x1, blocking collectives, shards(): square_total = lax.psum(jnp.sum(gated * gated, axis=1), 'head')  13.7 us
    dot_general x1, matrix products, shards(): jnp.einsum('chts,cshp->cthp', decays * scores[:, None, :, :], group_x, pr...  12 us
    ppermute x2, starting transfers between devices, shifted(): return lax.ppermute(x, axis, pairs)  9.29 us
  transfers between devices with their start and end apart: 5, of which 3 were waited for; matrix products, arithmetic and copies ran while one was open for 9% of the time, Pallas kernels for 0%

commit v1 on v0

--- a/solution.py
+++ b/solution.py
@@ -70,7 +70,9 @@
     lag_count = conv_x.shape[0] - 1
     device = lax.axis_index("seq")
     first_row = device * rows_here
-    piece = lax.all_gather(tokens, "head", axis=1, tiled=True)
+    piece = jnp.concatenate(
+        lax.all_to_all(jnp.stack([tokens] * lax.axis_size("head")), "head", 0, 0), axis=1
+    )
 
     def partial_product(matrix):
         return jnp.dot(piece, matrix, preferred_element_type=jnp.float32)

time: 349 us -> 390 us (1.12)
  waiting for transfers between devices: 205 us -> 236 us
  starting transfers between devices: 9.41 us -> 14.7 us
    all_to_all x0 -> x1, waiting for transfers between devices: none -> 92.6 us  [shards(): lax.all_to_all(jnp.stack([tokens] * lax.axis_size('head')), 'head', 0, 0)]
    all_gather x1 -> x0, waiting for transfers between devices: 58.4 us -> none  [shards(): piece = lax.all_gather(tokens, 'head', axis=1, tiled=True)]
    all_to_all x0 -> x1, starting transfers between devices: none -> 9.13 us  [shards(): lax.all_to_all(jnp.stack([tokens] * lax.axis_size('head')), 'head', 0, 0)]
  transfers between devices with their start and end apart: 5 -> 5, of which waited for: 3 -> 3; matrix products, arithmetic and copies ran while one was open for 9% -> 8% of each run, Pallas kernels for 0% -> 0%
where the time goes in v1:
time: 390 us; the launch traced here: 388 us
  waiting for transfers between devices  236 us (61%)
  matrix products  46.1 us (12%)
  blocking collectives  36.3 us (9%)
  local copies, waits for them, and re-layouts  21.7 us (6%)
  other arithmetic  19.2 us (5%)
  starting transfers between devices  14.7 us (4%)
  between operations  14.3 us (4%)
    reduce_scatter x1, waiting for transfers between devices, shards(): lax.psum_scatter(partial_out, 'head', scatter_dimension=1, tiled=True)  126 us
    all_to_all x1, waiting for transfers between devices, shards(): lax.all_to_all(jnp.stack([tokens] * lax.axis_size('head')), 'head', 0, 0)  92.6 us
    all_gather x1, blocking collectives, carried_in(): gathered = jax.tree.map(lambda a: lax.all_gather(a, axis), part)  22.6 us
    dot_general x4, matrix products, partial_product(): return jnp.dot(piece, matrix, preferred_element_type=jnp.float32)  20.1 us
    all_gather x1, waiting for transfers between devices, carried_in(): gathered = jax.tree.map(lambda a: lax.all_gather(a, axis), part)  17.7 us
    psum x1, blocking collectives, shards(): square_total = lax.psum(jnp.sum(gated * gated, axis=1), 'head')  13.7 us
    dot_general x1, matrix products, shards(): jnp.einsum('chts,cshp->cthp', decays * scores[:, None, :, :], group_x, pr...  12 us
    all_to_all x1, starting transfers between devices, shards(): lax.all_to_all(jnp.stack([tokens] * lax.axis_size('head')), 'head', 0, 0)  9.13 us
  transfers between devices with their start and end apart: 5, of which 3 were waited for; matrix products, arithmetic and copies ran while one was open for 8% of the time, Pallas kernels for 0%

profile of v1, /device:TPU:1, one launch (start us, length us, event | category | flops | bytes accessed | tf_op | source)
XLA Modules:
  0.0 388.4 jit_solution(1629076857514512629)
XLA Ops:
  7.2 1.4 copy.67
  8.6 2.5 stack.6
  11.1 9.1 %all-to-all-start = ((bf16[8,1024,256]{1,2,0:T(8,128)(2,1)}), bf16[8,1024,256]{1,2,0:T(8,128)(2,1)}, u32[]{:S(2)}, u32[]{:S(2)}) async-start(bf16[8,1024,256]{1,2,0:T(8,128)(2,1)} %stack.6), calls=%async_computation | async-start | bytes 8388608 | tf_op jit(solution)/shard_map/all_to_all | solution.py:74
  20.3 0.7 dynamic_slice.17
  21.0 0.8 broadcast_select_fusion
  21.7 0.6 slice.151
  22.3 0.2 fusion.60
  22.5 0.7 pad_add_fusion.1
  23.2 0.2 slice_reduce_fusion.1
  23.4 0.8 fusion.53
  24.4 92.6 %all-to-all-done = bf16[8,1024,256]{1,2,0:T(8,128)(2,1)} async-done(((bf16[8,1024,256]{1,2,0:T(8,128)(2,1)}), bf16[8,1024,256]{1,2,0:T(8,128)(2,1)}, u32[]{:S(2)}, u32[]{:S(2)}) %all-to-all-start) | async-done | bytes 4194336 | tf_op jit(solution)/shard_map/all_to_all | solution.py:74
  117.1 3.8 convolution_convert_fusion.1
  120.9 3.6 collective-permute-start.1
  124.5 2.9 negate_multiply_fusion
  127.4 2.3 reduce-window.6
  129.7 0.1 copy.70
  129.9 0.1 exponential_select_fusion
  130.0 0.2 slice_reduce_fusion
  130.1 5.2 %convolution_convert_fusion = bf16[1024,512]{1,0:T(8,128)(2,1)S(1)} fusion(bf16[1024,2048]{0,1:T(8,128)(2,1)} %bitcast.3, bf16[2048,512]{1,0:T(8,128)(2,1)} %param.20), kind=kOutput, calls=%fused_computation.32 | convolution fusion | flops 2148007936 | bytes 7340032 | tf_op jit(solution)/shard_map/dot_general | solution.py:78
  135.4 0.1 exponential_select_fusion.1
  135.6 1.9 collective-permute-start
  137.5 0.1 maximum_convert_fusion.1
  137.7 1.3 multiply_convert_fusion.3
  139.0 0.7 fusion.58
  139.8 0.3 maximum_convert_fusion
  140.1 3.1 fusion.37
  143.3 2.9 copy.68
  146.2 3.2 reshape.172
  149.4 3.8 broadcast_multiply_fusion
  153.2 1.3 fusion.18
  154.5 1.1 multiply_add_fusion
  155.7 0.1 mul.359
  155.8 0.2 compare_and_fusion
  156.1 22.6 %all-gather = f32[32,1,8]{2,1,0:T(1,128)S(1)} all-gather(f32[1,1,8]{2,1,0:T(1,128)S(1)} %get-tuple-element.93), channel_id=1, replica_groups=mesh['seq'=32,'head'=8] {'seq'}, dimensions={0}, use_global_device_ids=true | all-gather | bytes 1056 | tf_op jit(solution)/shard_map/all_gather | solution.py:20
  178.8 1.2 fusion.63
  180.1 12.0 %fusion = f32[4,8,64,256]{3,2,1,0:T(8,128)} fusion(f32[4,256,256]{2,1,0:T(8,128)S(1)} %fusion.63, f32[4,8,256]{2,1,0:T(8,128)S(1)} %add_bitcast_fusion.1, pred[4,256,256]{2,1,0:T(8,128)(4,1)S(1)} %compare_and_fusion, f32[4,256,8,64]{1,0,3,2:T(4,128)} %get-tuple-element.69), kind=kOutput, calls=%fused_computation.2 | convolution fusion | flops 1619001344 | bytes 5537792 | tf_op jit(solution)/shard_map/chts,cshp->cthp/dot_general | solution.py:116
  192.1 17.7 %all-gather.3.cloned.1.call-done = f32[32,8,64,128]{3,2,1,0:T(8,128)} async-done(((f32[1,8,64,128]{3,2,1,0:T(8,128)}), f32[32,8,64,128]{3,2,1,0:T(8,128)}) %all-gather.3.cloned.1.call-update) | async-done | bytes 8388624 | tf_op jit(solution)/shard_map/all_gather | solution.py:20
  209.8 1.1 while.12
  209.9 1.1 bitcast_add_fusion.7
  210.9 4.3 %bitcast_add_fusion.1 = f32[4,256,8,64]{1,3,2,0:T(8,128)} fusion(f32[4,8,64,256]{3,2,1,0:T(8,128)} %fusion, bf16[4,256,128,1]{2,1,3,0:T(8,128)(2,1)} %bitcast.117, f32[1,8,64,128]{3,2,1,0:T(8,128)} %get-tuple-element.60, f32[1,8,64,128]{3,2,1,0:T(8,128)} %get-tuple-element.61, f32[1,8,64,128]{3,2,1,0:T(8,128)} %get-tuple-element.62, ...), kind=kOutput, calls=%fused_computation.24 | convolution fusion | flops 807665664 | bytes 5537936 | tf_op jit(solution)/shard_map/ctn,chpn->cthp/dot_general | solution.py:140
  215.3 3.8 copy.82
  219.1 4.8 %reshape.183 = f32[1024,512]{1,0:T(8,128)} reshape(f32[4,256,8,64]{3,2,1,0:T(8,128)} %copy.82) | data formatting | bytes 4194304 | tf_op jit(solution)/shard_map/reshape | solution.py:144
  223.9 8.1 %multiply_reduce_fusion = (f32[1024]{0:T(1024)S(1)}, f32[1024,512]{1,0:T(8,128)}) fusion(f32[1024,512]{1,0:T(8,128)} %reshape.183, f32[1024,512]{1,0:T(8,128)} %fusion.37, f32[512]{0:T(512)S(1)} %mul.359, bf16[1024,2048]{0,1:T(8,128)(2,1)} %bitcast.3, bf16[2048,512]{1,0:T(8,128)(2,1)} %param.19), kind=kOutput, calls=%fused_computation.29 | convolution fusion | flops 2152201216 | bytes 12589056 | tf_op jit(solution)/shard_map/dot_general | solution.py:78
  232.0 13.7 %psum.7 = f32[1024]{0:T(1024)S(1)} all-reduce(f32[1024]{0:T(1024)S(1)} %get-tuple-element.57), channel_id=1, replica_groups=mesh['seq'=32,'head'=8] {'head'}, use_global_device_ids=true, to_apply=%region_5.6 | all-reduce | flops 1024 | bytes 8192 | tf_op jit(solution)/shard_map/psum | solution.py:148
  245.7 7.2 %fusion.21 = f32[1024,2048]{1,0:T(8,128)} fusion(bf16[512,2048]{1,0:T(8,128)(2,1)S(1)} %copy-done, f32[1024,512]{1,0:T(8,128)} %get-tuple-element.58, f32[512]{0:T(512)S(1)} %copy-done.2, f32[1024]{0:T(1024)S(1)} %add_rsqrt_fusion), kind=kOutput, calls=%fused_computation.36 | convolution fusion | flops 2149056512 | bytes 12589056 | tf_op jit(solution)/shard_map/dot_general | solution.py:151
  253.0 0.9 fusion.42
  253.8 125.7 %reduce-scatter.2.cloned.1.call-done = f32[1024,256]{1,0:T(8,128)} async-done(((f32[1024,2048]{1,0:T(8,128)}), f32[1024,256]{1,0:T(8,128)}) %reduce-scatter.2.cloned.1.call-update) | async-done | bytes 1048592 | tf_op jit(solution)/shard_map/reduce_scatter | solution.py:152
  379.5 2.1 convert_element_type.37
  (51 shorter events, 0.8 us)
Async XLA Ops:
  7.2 238.5 %copy-start = (bf16[512,2048]{1,0:T(8,128)(2,1)S(1)}, bf16[512,2048]{1,0:T(8,128)(2,1)}, u32[]{:S(2)}) copy-start(bf16[512,2048]{1,0:T(8,128)(2,1)} %param.31) | copy-start | bytes 6291460
  11.1 13.3 %copy-start.4 = (f32[4,256]{1,0:T(4,128)S(1)}, f32[4,256]{1,0:T(4,128)}, u32[]{:S(2)}) copy-start(f32[4,256]{1,0:T(4,128)} %param.24) | copy-start | bytes 12292
  11.1 13.3 %copy-start.3 = (f32[4,512]{1,0:T(4,128)S(1)}, f32[4,512]{1,0:T(4,128)}, u32[]{:S(2)}) copy-start(f32[4,512]{1,0:T(4,128)} %param.23) | copy-start | bytes 24580
  11.1 106.0 %all-to-all-start = ((bf16[8,1024,256]{1,2,0:T(8,128)(2,1)}), bf16[8,1024,256]{1,2,0:T(8,128)(2,1)}, u32[]{:S(2)}, u32[]{:S(2)}) async-start(bf16[8,1024,256]{1,2,0:T(8,128)(2,1)} %stack.6), calls=%async_computation | async-start | bytes 8388608 | tf_op jit(solution)/shard_map/all_to_all | solution.py:74
  20.2 189.6 %all-gather.3.cloned.1.call-start = ((), (), s32[]{:S(2)}) async-start(), calls=%async_computation.2 | async-start | bytes 8650752 | tf_op jit(solution)/shard_map/all_gather | solution.py:20
  117.0 7.4 %copy-start.1 = (bf16[2048,8]{0,1:T(8,128)(2,1)S(1)}, bf16[2048,8]{0,1:T(8,128)(2,1)}, u32[]{:S(2)}) copy-start(bf16[2048,8]{0,1:T(8,128)(2,1)} %param.22) | copy-start | bytes 98308
  117.0 7.4 %copy-start.6 = (f32[8]{0:T(128)S(1)}, f32[8]{0:T(128)}, u32[]{:S(2)}) copy-start(f32[8]{0:T(128)} %param.28) | copy-start | bytes 100
  117.1 7.5 %copy-start.7 = (f32[8]{0:T(128)S(1)}, f32[8]{0:T(128)}, u32[]{:S(2)}) copy-start(f32[8]{0:T(128)} %param.27) | copy-start | bytes 100
  120.9 16.6 %collective-permute-start.1 = (bf16[3,256]{1,0:T(4,128)(2,1)S(1)}, bf16[3,256]{1,0:T(4,128)(2,1)S(1)}, u32[]{:S(2)}, u32[]{:S(2)}) collective-permute-start(bf16[3,256]{1,0:T(4,128)(2,1)S(1)} %slice.175), channel_id=1, source_target_pairs={{0,8},{8,16},{16,24},{24,32},{32,40},{40,48},{48,56},{56,64},{64,7... | collective-permute-start | bytes 4616 | tf_op jit(solution)/shard_map/ppermute | solution.py:15
  130.1 7.5 %copy-start.8 = (f32[256]{0:T(256)S(1)}, f32[256]{0:T(256)}, u32[]{:S(2)}) copy-start(f32[256]{0:T(256)} %param.26) | copy-start | bytes 3076
  135.6 4.2 %collective-permute-start = (bf16[3,512]{1,0:T(4,128)(2,1)S(1)}, bf16[3,512]{1,0:T(4,128)(2,1)S(1)}, u32[]{:S(2)}, u32[]{:S(2)}) collective-permute-start(bf16[3,512]{1,0:T(4,128)(2,1)S(1)} %slice.164), channel_id=1, source_target_pairs={{0,8},{8,16},{16,24},{24,32},{32,40},{40,48},{48,56},{56,64},{64,7... | collective-permute-start | bytes 9224 | tf_op jit(solution)/shard_map/ppermute | solution.py:15
  139.0 1.1 copy-start.5
  153.2 2.4 copy-start.9
  155.5 224.0 %reduce-scatter.2.cloned.1.call-start = ((), (), s32[]{:S(2)}) async-start(), calls=%async_computation.3 | async-start | bytes 9437184 | tf_op jit(solution)/shard_map/reduce_scatter | solution.py:152
  223.9 21.8 %copy-start.2 = (f32[512]{0:T(512)S(1)}, f32[512]{0:T(512)}, u32[]{:S(2)}) copy-start(f32[512]{0:T(512)} %param.30) | copy-start | bytes 6148
Sparse Core Ops, SparseCore 0:
  155.7 54.1 all-gather.2
  253.1 126.4 reduce-scatter.1
